TPU v7x, 512 devices: a whole 4x8x8 slice. The times are simulated.
512 devices in a mesh: src: 128 (over y, z, core), freq: 4 (over x).
Axes of the slice: x: 4, y: 8, z: 8, core: 2. Of those that a mesh axis runs over, the one named last changes fastest.
Arguments:
- pupil_block: bfloat16 [32768, 1024], P('src'), may hold values from -6 to 6
- source_on: int32 [32768], P('src'), may hold values 0 or 1
- offsets: int32 [2, 32768], P(None, 'src'), may hold values from 0 to 96, as said below
- omega: bfloat16 [32768, 64], P('src'), may hold values from -6 to 6
Outputs:
- kernels: float32 [16384, 64], P('freq')
Inputs may be any that keep to these rules, and one draw needn't show every extreme that they name: offsets[0, s] and offsets[1, s] place source point s's whole window inside the grid.
All inputs are finite; a program needn't handle non-finite values. No bound on the sum of `source_on` on one device may be relied on, other than what follows from the above.
Results may differ from a plain program's by a relative error of at most 0.0033.
Values may be sent and summed in bfloat16 or wider, within the bound.
A program may use at most 64 MiB of HBM per device.

v0:
```python
import functools

import jax
import jax.numpy as jnp
from jax import lax
from jax.experimental import pallas as pl
from jax.experimental.pallas import tpu as pltpu
from jax.sharding import Mesh
from jax.sharding import PartitionSpec as P

G = 128
PB = 32
ITERS = 3
LANES = 128
SRC = ("src_0", "src_1", "src_2")
MESH_ID = pl.DeviceIdType.MESH


def split2(value):
    high = value.astype(jnp.bfloat16)
    low = (value - high.astype(jnp.float32)).astype(jnp.bfloat16)
    return high, low


def dot_nn(left, right):
    return lax.dot_general(
        left, right, (((1,), (0,)), ((), ())), preferred_element_type=jnp.float32
    )


def dot_nt(left, right):
    return lax.dot_general(
        left, right, (((1,), (1,)), ((), ())), preferred_element_type=jnp.float32
    )


def apply_factor(inv_high, inv_low, value):
    high, low = split2(value)
    return dot_nn(inv_high, high) + (dot_nn(inv_high, low) + dot_nn(inv_low, high))


def place_windows(pupil_ref, off_ref, on_ref, meta_ref, a_ref, a_row, base_row, rows):
    points = pupil_ref.shape[0]
    per = LANES // PB
    chunk = 16

    def spread(line):
        return jnp.transpose(jnp.broadcast_to(line, (LANES, points)))

    meta_ref[0] = spread(off_ref[0:1, :])
    meta_ref[1] = spread(off_ref[1:2, :])
    meta_ref[2] = spread(on_ref[0:1, :])

    def block(index, carry):
        s0 = pl.multiple_of(index * chunk, chunk)
        row_off = meta_ref[0, pl.ds(s0, chunk), :]
        col_off = meta_ref[1, pl.ds(s0, chunk), :]
        lit = meta_ref[2, pl.ds(s0, chunk), :].astype(jnp.float32)
        lane = lax.broadcasted_iota(jnp.int32, (chunk, LANES), 1)
        shift = jnp.clip(base_row - row_off, -rows, PB) + rows
        window = pupil_ref[pl.ds(s0, chunk), :].astype(jnp.float32)
        tiles = [None] * (rows // per)
        tiles += [window[:, i * LANES : (i + 1) * LANES] * lit for i in range(PB // per)]
        tiles += [None] * (rows // per)
        zero = jnp.zeros((chunk, LANES), jnp.float32)

        def pick(mask, taken, kept):
            if taken is None and kept is None:
                return None
            return jnp.where(mask, zero if taken is None else taken, zero if kept is None else kept)

        kept_tiles = rows // per + 1
        for bit in reversed(range(((rows + PB) // per).bit_length())):
            step = 1 << bit
            mask = (shift & (step * per)) != 0
            count = kept_tiles + step - 1
            at = lambda i: tiles[i] if i < len(tiles) else None
            tiles = [pick(mask, at(i + step), at(i)) for i in range(count)]
        for step in (2, 1):
            mask = (shift & step) != 0
            turned = [None if t is None else pltpu.roll(t, LANES - PB * step, 1) for t in tiles]
            turned.append(None)
            inside = lane < LANES - PB * step
            moved = [pick(inside, turned[i], turned[i + 1]) for i in range(len(tiles))]
            tiles = [pick(mask, moved[i], tiles[i]) for i in range(len(tiles))]
        tiles = tiles[: rows // per]
        for bit in range(LANES.bit_length() - 1):
            mask = (col_off & (1 << bit)) != 0
            tiles = [jnp.where(mask, pltpu.roll(t, 1 << bit, 1), t) for t in tiles]
        inner = lane - col_off
        covered = (inner >= 0) & (inner < PB)
        for row in range(rows):
            tile, group = tiles[row // per], row % per
            if group:
                tile = pltpu.roll(tile, LANES - PB * group, 1)
            a_ref[pl.ds(a_row + s0, chunk), row * LANES : (row + 1) * LANES] = jnp.where(
                covered, tile, 0.0
            ).astype(jnp.bfloat16)
        return carry

    lax.fori_loop(0, points // chunk, block, 0)


def inverse_factor(packed, size):
    half = size // 2
    whole = jnp.concatenate([pltpu.roll(packed, size, 1), packed], axis=0)
    lane = lax.broadcasted_iota(jnp.int32, (8, LANES), 1)
    sub = lax.broadcasted_iota(jnp.int32, (8, LANES), 0)
    tiles = []
    for t in range(size // 8):
        eye = jnp.where(lane == sub + 8 * t, 1.0, 0.0)
        tiles.append(jnp.where(lane < size, eye, whole[8 * t : 8 * t + 8]))
    for k in range(size):
        home, inside = k // 8, k % 8
        line = tiles[home][inside : inside + 1, :]
        scaled = line * (1.0 / line[:, size + k : size + k + 1])
        for t in range(home, size // 8):
            column = tiles[t][:, size + k : size + k + 1]
            if t == home:
                column = jnp.where(sub[:, :1] > inside, column, 0.0)
            tiles[t] = tiles[t] - column * scaled
    done = []
    for t in range(size // 8):
        pivot = jnp.sum(jnp.where(lane == sub + (8 * t + size), tiles[t], 0.0), axis=1, keepdims=True)
        done.append(tiles[t] * lax.rsqrt(pivot))
    return jnp.concatenate(done, axis=0)[:, :size]


def kernel(
    sizes, pupil_ref, on_ref, off_ref, omega_ref, out_ref,
    pupil_far, on_far, off_far, meta, a_ref, cpl_own, cpl_far,
    part, got1, sum1, got2, sum2, img, split, gram_out, gram_in, w_far, w_far_in, w_own, w_in,
    setup_send, setup_recv, st_send, st_recv, gram_send, gram_recv, w_send, w_recv, x_send, x_recv,
    c_send, c_recv, f_send, f_recv,
):
    n_y, n_z, n_c, n_x = sizes
    my_y, my_z = lax.axis_index("src_0"), lax.axis_index("src_1")
    my_c, my_x = lax.axis_index("src_2"), lax.axis_index("freq")
    other = {"src_2": 1 - my_c}
    rows = G // (n_x * n_c)
    size = omega_ref.shape[0]
    points = pupil_ref.shape[0]
    half = rows * G // 2
    axes = ("src_0", "src_1")
    count = (n_y, n_z)
    mine = (my_y, my_z)

    def offsets_far_first(n):
        return sorted(range(1, n), key=lambda d: (-min(d, n - d), d))

    group = [(dx, dc) for dx in range(n_x) for dc in range(n_c) if dx or dc]

    def group_peer(dx, dc):
        peer_x = lax.rem(my_x + dx, n_x)
        peer_c = lax.rem(my_c + dc, n_c)
        return peer_x, peer_c

    barrier = pltpu.get_barrier_semaphore()
    for a in range(2):
        for d in range(1, count[a]):
            pl.semaphore_signal(
                barrier, inc=1, device_id={axes[a]: lax.rem(mine[a] + d, count[a])},
                device_id_type=MESH_ID,
            )
    for dx, dc in group:
        peer_x, peer_c = group_peer(dx, dc)
        pl.semaphore_signal(
            barrier, inc=1, device_id={"freq": peer_x, "src_2": peer_c}, device_id_type=MESH_ID
        )
    pl.semaphore_wait(barrier, n_y - 1 + n_z - 1 + len(group))

    def remote(src, dst, send, recv, device):
        return pltpu.make_async_remote_copy(
            src_ref=src, dst_ref=dst, send_sem=send, recv_sem=recv,
            device_id=device, device_id_type=MESH_ID,
        )

    setup = [
        remote(src, dst, setup_send.at[i], setup_recv.at[i], other)
        for i, (src, dst) in enumerate(
            ((off_ref, off_far), (on_ref, on_far), (omega_ref, cpl_far.at[0]), (pupil_ref, pupil_far))
        )
    ]
    for copy in setup:
        copy.start()
    base_row = my_x * (rows * n_c) + my_c * rows
    place_windows(pupil_ref, off_ref, on_ref, meta, a_ref, 0, base_row, rows)
    for copy in setup:
        copy.wait()
    place_windows(pupil_far, off_far, on_far, meta, a_ref, points, base_row, rows)

    def stage(it, which, h):
        along = h if which != 1 else 1 - h
        n, me, name = count[along], mine[along], axes[along]
        copies = []
        for d in offsets_far_first(n):
            peer = lax.rem(me + d, n)
            if which == 0:
                src, dst = part.at[it, h, peer], got1.at[it, h, me]
            elif which == 1:
                src, dst = sum1.at[it, h], got2.at[it, h, me]
            else:
                src, dst = sum2.at[it, h], img.at[it, h, me]
            slot = (which * 2 + h) * n
            copies.append(
                (remote(src, dst, st_send.at[it, slot + peer], st_recv.at[it, slot + me], {name: peer}), d)
            )
        for copy, d in copies:
            copy.start()
        return copies

    def arrive(it, which, h, copies):
        along = h if which != 1 else 1 - h
        n, me, name = count[along], mine[along], axes[along]
        into = (got1, got2, img)[which]
        for d in offsets_far_first(n):
            peer = lax.rem(me + d, n)
            slot = (which * 2 + h) * n
            remote(
                into.at[it, h, peer], into.at[it, h, peer], st_send.at[it, slot + peer],
                st_recv.at[it, slot + peer], {name: peer},
            ).wait_recv()
        pending.extend(copy for copy, d in copies)

    pending = []
    eye_low = None
    for it in range(ITERS):
        last = it == ITERS - 1
        left_own = omega_ref[...] if it == 0 else cpl_own[it]
        if it > 0:
            remote(cpl_own.at[it], cpl_far.at[it], c_send.at[it], c_recv.at[it], other).wait_recv()
        left_far = cpl_far[it]
        flights = []
        width = min(256, half)
        for h in range(2):
            for j in range(half // width):
                cols = slice(h * half + j * width, h * half + (j + 1) * width)
                total = dot_nn(left_own, a_ref[0:points, cols]) + dot_nn(
                    left_far, a_ref[points : 2 * points, cols]
                )
                part[it, h, :, :, j * width : (j + 1) * width] = total.reshape(
                    count[h], size // count[h], width
                )
            flights.append(stage(it, 0, h))
        second = []
        for h in range(2):
            me, n = mine[h], count[h]
            got1[it, h, me] = part[it, h, me]
            arrive(it, 0, h, flights[h])
            total = got1[it, h, 0]
            for p in range(1, n):
                total = total + got1[it, h, p]
            sum1[it, h] = total
            second.append(stage(it, 1, h))
            got2[it, h, mine[1 - h]] = total
        third = []
        for h in range(2):
            n = count[1 - h]
            arrive(it, 1, h, second[h])
            total = got2[it, h, 0]
            for p in range(1, n):
                total = total + got2[it, h, p]
            sum2[it, h] = total
            third.append(stage(it, 2, h))
            img[it, h, mine[h]] = total
        for h in range(2):
            arrive(it, 2, h, third[h])
            high, low = split2(img[it, h].reshape(size, half))
            split[0:size, h * half : (h + 1) * half] = high
            split[size : 2 * size, h * half : (h + 1) * half] = low
        if last:
            final = remote(img.at[it], img.at[it + 1], f_send.at[0], f_recv.at[0], other)
            final.start()
        both = split[...]
        square = dot_nt(both, both)
        square = square[:size] + square[size:]
        square = square + pltpu.roll(square, size, 1)
        lane = lax.broadcasted_iota(jnp.int32, (size // 2, LANES), 1)
        packed = jnp.where(lane < size, square[: size // 2], square[size // 2 :])
        gram_out[it] = packed
        my_slot = my_x * n_c + my_c
        gram_in[it, my_slot] = packed
        for i, (dx, dc) in enumerate(group):
            peer_x, peer_c = group_peer(dx, dc)
            copy = remote(
                gram_out.at[it], gram_in.at[it, my_slot], gram_send.at[it, i],
                gram_recv.at[it, my_slot], {"freq": peer_x, "src_2": peer_c},
            )
            copy.start()
            pending.append(copy)
        if not last:
            far = dot_nt(both, a_ref[points : 2 * points, :])
            w_far[it] = far[:size] + far[size:]
            swap = remote(w_far.at[it], w_far_in.at[it], w_send.at[it], w_recv.at[it], other)
            swap.start()
            pending.append(swap)
            own = dot_nt(both, a_ref[0:points, :])
            own = own[:size] + own[size:]
            swap.wait_recv()
            own = own + w_far_in[it]
            w_own[it] = own
            w_in[it, my_x] = own
            for d in offsets_far_first(n_x):
                peer = lax.rem(my_x + d, n_x)
                copy = remote(
                    w_own.at[it], w_in.at[it, my_x], x_send.at[it, d], x_recv.at[it, my_x],
                    {"freq": peer},
                )
                copy.start()
                pending.append(copy)
        for dx, dc in group:
            peer_x, peer_c = group_peer(dx, dc)
            slot = peer_x * n_c + peer_c
            remote(
                gram_out.at[it], gram_in.at[it, slot], gram_send.at[it, 0], gram_recv.at[it, slot],
                {"freq": peer_x, "src_2": peer_c},
            ).wait_recv()
        total = gram_in[it, 0]
        for p in range(1, n_x * n_c):
            total = total + gram_in[it, p]
        inv_high, inv_low = split2(inverse_factor(total * (1.0 / (G * G)), size))
        if not last:
            for d in offsets_far_first(n_x):
                peer = lax.rem(my_x + d, n_x)
                remote(
                    w_own.at[it], w_in.at[it, peer], x_send.at[it, d], x_recv.at[it, peer],
                    {"freq": peer},
                ).wait_recv()
            total = w_in[it, 0]
            for p in range(1, n_x):
                total = total + w_in[it, p]
            cpl_own[it + 1] = apply_factor(inv_high, inv_low, total).astype(jnp.bfloat16)
            copy = remote(
                cpl_own.at[it + 1], cpl_far.at[it + 1], c_send.at[it + 1], c_recv.at[it + 1], other
            )
            copy.start()
            pending.append(copy)
        else:
            final.wait()
            width = min(256, half)
            for c in range(2):
                slot = it + jnp.where(my_c == c, 0, 1)
                for h in range(2):
                    for j in range(half // width):
                        value = img[slot, h, :, :, j * width : (j + 1) * width].reshape(size, width)
                        start = (c * 2 + h) * half + j * width
                        out_ref[:, start : start + width] = apply_factor(inv_high, inv_low, value)
    for copy in pending:
        copy.wait_send()


def shards(pupil_block, source_on, offsets, omega):
    points = pupil_block.shape[0]
    size = omega.shape[1]
    n_y, n_z, n_c = (lax.axis_size(name) for name in SRC)
    n_x = lax.axis_size("freq")
    rows = G // (n_x * n_c)
    freqs = rows * G
    half = freqs // 2
    ky, kz = size // n_y, size // n_z
    assert n_y == n_z and n_c == 2
    f32, bf16, i32 = jnp.float32, jnp.bfloat16, jnp.int32
    vmem = pltpu.VMEM
    dma = pltpu.SemaphoreType.DMA
    scratch = [
        vmem((points, PB * PB), bf16), vmem((1, points), i32), vmem((2, points), i32),
        vmem((3, points, LANES), i32),
        vmem((2 * points, freqs), bf16),
        vmem((ITERS, size, points), bf16), vmem((ITERS, size, points), bf16),
        vmem((ITERS, 2, n_y, ky, half), f32), vmem((ITERS, 2, n_y, ky, half), f32),
        vmem((ITERS, 2, ky, half), f32), vmem((ITERS, 2, n_z, ky, half), f32),
        vmem((ITERS, 2, ky, half), f32), vmem((ITERS + 1, 2, n_y, ky, half), f32),
        vmem((2 * size, freqs), bf16),
        vmem((ITERS, size // 2, LANES), f32), vmem((ITERS, n_x * n_c, size // 2, LANES), f32),
        vmem((ITERS, size, points), f32), vmem((ITERS, size, points), f32),
        vmem((ITERS, size, points), f32), vmem((ITERS, n_x, size, points), f32),
        dma((4,)), dma((4,)), dma((ITERS, 6 * n_y)), dma((ITERS, 6 * n_y)),
        dma((ITERS, n_x * n_c)), dma((ITERS, n_x * n_c)), dma((ITERS,)), dma((ITERS,)),
        dma((ITERS, n_x)), dma((ITERS, n_x)), dma((ITERS,)), dma((ITERS,)), dma((1,)), dma((1,)),
    ]
    out = pl.pallas_call(
        functools.partial(kernel, (n_y, n_z, n_c, n_x)),
        out_shape=jax.ShapeDtypeStruct((size, freqs * n_c), f32),
        in_specs=[pl.BlockSpec(memory_space=pltpu.VMEM)] * 4,
        out_specs=pl.BlockSpec(memory_space=pltpu.VMEM),
        scratch_shapes=scratch,
        compiler_params=pltpu.CompilerParams(
            collective_id=0, has_side_effects=True, vmem_limit_bytes=60 * 1024 * 1024
        ),
    )(pupil_block, source_on.reshape(1, points), offsets, omega.T)
    return out.T


def solution(mesh):
    split = Mesh(
        mesh.devices.reshape(8, 8, 2, mesh.shape["freq"]), ("src_0", "src_1", "src_2", "freq")
    )
    return jax.shard_map(
        shards,
        mesh=split,
        in_specs=(P(SRC, None), P(SRC), P(None, SRC), P(SRC, None)),
        out_specs=P("freq", None),
        check_vma=False,
    )
```

profile of v0, /device:TPU:1, one launch (start us, length us, event | category | flops | bytes accessed | tf_op | source)
XLA Modules:
  0.0 153.3 jit_solution(14531169222850671521)
XLA Ops:
  0.0 151.1 %shard_map.46 = f32[64,4096]{1,0:T(8,128)} custom-call(bf16[256,1024]{1,0:T(8,128)(2,1)} %pupil_ref.1, s32[1,256]{1,0:T(1,128)} %bitcast.5, s32[2,256]{1,0:T(2,128)} %off_ref.1, bf16[64,256]{1,0:T(8,128)(2,1)} %bitcast.4), custom_call_target="tpu_custom_call" | custom-call | tf_op jit(solution)/shard_map/pallas_call | solution.py:381
  151.1 2.3 %copy.6 = f32[4096,64]{0,1:T(8,128)} copy(f32[4096,64]{0,1:T(8,128)} %bitcast.3) | data formatting | bytes 2097152
where the time goes:
time: 154 us; the launch traced here: 153 us
  Pallas kernels  151 us (98%)
  local copies, waits for them, and re-layouts  2.27 us (1%)
    pallas_call x1, Pallas kernels, shards(): pl.pallas_call(functools.partial(kernel, (n_y, n_z, n_c, n_x)), out_shape...  151 us

commit v1 on v0

--- a/solution.py
+++ b/solution.py
@@ -12,6 +12,8 @@
 PB = 32
 ITERS = 3
 LANES = 128
+LEVELS = 32700.0
+TINY = 1e-30
 SRC = ("src_0", "src_1", "src_2")
 MESH_ID = pl.DeviceIdType.MESH
 
@@ -34,15 +36,38 @@
     )
 
 
-def apply_factor(inv_high, inv_low, value):
-    high, low = split2(value)
+def apply_factor(inv_high, inv_low, high, low):
     return dot_nn(inv_high, high) + (dot_nn(inv_high, low) + dot_nn(inv_low, high))
+
+
+def encode(value):
+    top = jnp.maximum(jnp.max(jnp.abs(value), axis=1, keepdims=True), TINY)
+    level = lax.round(value * (LEVELS / top), lax.RoundingMethod.TO_NEAREST_EVEN)
+    return level.astype(jnp.int32), top
+
+
+def diagonal(rows):
+    shape = (rows, LANES)
+    return lax.broadcasted_iota(jnp.int32, shape, 1) == lax.broadcasted_iota(jnp.int32, shape, 0)
+
+
+def column_to_line(top):
+    rows = top.shape[0]
+    wide = jnp.broadcast_to(top, (rows, LANES))
+    return jnp.sum(jnp.where(diagonal(rows), wide, 0.0), axis=0, keepdims=True)
+
+
+def decode(level, line):
+    rows = level.shape[0]
+    wide = jnp.broadcast_to(line, (rows, LANES))
+    top = jnp.sum(jnp.where(diagonal(rows), wide, 0.0), axis=1, keepdims=True)
+    return level.astype(jnp.int32).astype(jnp.float32) * (top * (1.0 / LEVELS))
 
 
 def place_windows(pupil_ref, off_ref, on_ref, meta_ref, a_ref, a_row, base_row, rows):
     points = pupil_ref.shape[0]
     per = LANES // PB
-    chunk = 16
+    chunk = min(64, points)
 
     def spread(line):
         return jnp.transpose(jnp.broadcast_to(line, (LANES, points)))
@@ -102,23 +127,52 @@
 
 
 def inverse_factor(packed, size):
-    half = size // 2
     whole = jnp.concatenate([pltpu.roll(packed, size, 1), packed], axis=0)
-    lane = lax.broadcasted_iota(jnp.int32, (8, LANES), 1)
-    sub = lax.broadcasted_iota(jnp.int32, (8, LANES), 0)
+    full = (8, LANES)
+    lane = lax.broadcasted_iota(jnp.int32, full, 1)
+    sub = lax.broadcasted_iota(jnp.int32, full, 0)
     tiles = []
     for t in range(size // 8):
         eye = jnp.where(lane == sub + 8 * t, 1.0, 0.0)
         tiles.append(jnp.where(lane < size, eye, whole[8 * t : 8 * t + 8]))
-    for k in range(size):
-        home, inside = k // 8, k % 8
-        line = tiles[home][inside : inside + 1, :]
-        scaled = line * (1.0 / line[:, size + k : size + k + 1])
+    wide = 4
+    for k in range(0, size, wide):
+        home, first = k // 8, k % 8
+        columns = [
+            [jnp.broadcast_to(tiles[t][:, size + k + j : size + k + j + 1], full) for j in range(wide)]
+            for t in range(home, size // 8)
+        ]
+        lines = [jnp.broadcast_to(tiles[home][first + i : first + i + 1, :], full) for i in range(wide)]
+        block = [
+            [jnp.broadcast_to(columns[0][j][first + i : first + i + 1, :], full) for j in range(i + 1)]
+            for i in range(wide)
+        ]
+        ratio, scaled = {}, []
+        for p in range(wide):
+            inverse = 1.0 / block[p][p]
+            for i in range(p + 1, wide):
+                ratio[i, p] = block[i][p] * inverse
+                for j in range(p + 1, i + 1):
+                    block[i][j] = block[i][j] - ratio[i, p] * block[j][p]
+            for i in range(p + 1, wide):
+                lines[i] = lines[i] - ratio[i, p] * lines[p]
+            scaled.append(lines[p] * inverse)
         for t in range(home, size // 8):
-            column = tiles[t][:, size + k : size + k + 1]
+            own = columns[t - home]
+            taken = None
+            for p in range(wide):
+                weight = own[p]
+                for q in range(p):
+                    weight = weight - ratio[p, q] * own[q]
+                own[p] = weight
+                term = weight * scaled[p]
+                taken = term if taken is None else taken + term
+            updated = tiles[t] - taken
             if t == home:
-                column = jnp.where(sub[:, :1] > inside, column, 0.0)
-            tiles[t] = tiles[t] - column * scaled
+                updated = jnp.where(sub >= first + wide, updated, tiles[t])
+                for i in range(1, wide):
+                    updated = jnp.where(sub == first + i, lines[i], updated)
+            tiles[t] = updated
     done = []
     for t in range(size // 8):
         pivot = jnp.sum(jnp.where(lane == sub + (8 * t + size), tiles[t], 0.0), axis=1, keepdims=True)
@@ -129,7 +183,8 @@
 def kernel(
     sizes, pupil_ref, on_ref, off_ref, omega_ref, out_ref,
     pupil_far, on_far, off_far, meta, a_ref, cpl_own, cpl_far,
-    part, got1, sum1, got2, sum2, img, split, gram_out, gram_in, w_far, w_far_in, w_own, w_in,
+    level, level_top, part_q, part_s, got1_q, got1_s, sum1_q, sum1_s, got2_q, got2_s, sum2_q, sum2_s,
+    img_q, img_s, split, gram_out, gram_in, w_far, w_far_in, w_own, w_in,
     setup_send, setup_recv, st_send, st_recv, gram_send, gram_recv, w_send, w_recv, x_send, x_recv,
     c_send, c_recv, f_send, f_recv,
 ):
@@ -141,9 +196,11 @@
     size = omega_ref.shape[0]
     points = pupil_ref.shape[0]
     half = rows * G // 2
+    quarter = half // 2
     axes = ("src_0", "src_1")
     count = (n_y, n_z)
     mine = (my_y, my_z)
+    kept = size // n_y
 
     def offsets_far_first(n):
         return sorted(range(1, n), key=lambda d: (-min(d, n - d), d))
@@ -189,89 +246,105 @@
         copy.wait()
     place_windows(pupil_far, off_far, on_far, meta, a_ref, points, base_row, rows)
 
+    outgoing = ((part_q, part_s), (sum1_q, sum1_s), (sum2_q, sum2_s))
+    incoming = ((got1_q, got1_s), (got2_q, got2_s), (img_q, img_s))
+
+    def ring(which, h):
+        along = h if which != 1 else 1 - h
+        return count[along], mine[along], axes[along]
+
     def stage(it, which, h):
-        along = h if which != 1 else 1 - h
-        n, me, name = count[along], mine[along], axes[along]
-        copies = []
-        for d in offsets_far_first(n):
-            peer = lax.rem(me + d, n)
-            if which == 0:
-                src, dst = part.at[it, h, peer], got1.at[it, h, me]
-            elif which == 1:
-                src, dst = sum1.at[it, h], got2.at[it, h, me]
-            else:
-                src, dst = sum2.at[it, h], img.at[it, h, me]
-            slot = (which * 2 + h) * n
-            copies.append(
-                (remote(src, dst, st_send.at[it, slot + peer], st_recv.at[it, slot + me], {name: peer}), d)
-            )
-        for copy, d in copies:
-            copy.start()
-        return copies
-
-    def arrive(it, which, h, copies):
-        along = h if which != 1 else 1 - h
-        n, me, name = count[along], mine[along], axes[along]
-        into = (got1, got2, img)[which]
+        n, me, name = ring(which, h)
         for d in offsets_far_first(n):
             peer = lax.rem(me + d, n)
             slot = (which * 2 + h) * n
-            remote(
-                into.at[it, h, peer], into.at[it, h, peer], st_send.at[it, slot + peer],
-                st_recv.at[it, slot + peer], {name: peer},
-            ).wait_recv()
-        pending.extend(copy for copy, d in copies)
+            for i in range(2):
+                src = outgoing[which][i].at[it, h]
+                copy = remote(
+                    src.at[peer] if which == 0 else src, incoming[which][i].at[it, h, me],
+                    st_send.at[it, i, slot + peer], st_recv.at[it, i, slot + me], {name: peer},
+                )
+                copy.start()
+                pending.append(copy)
+        for i in range(2):
+            src = outgoing[which][i].at[it, h]
+            incoming[which][i][it, h, me] = src[me] if which == 0 else src[...]
+
+    def arrive(it, which, h):
+        n, me, name = ring(which, h)
+        for d in offsets_far_first(n):
+            peer = lax.rem(me + d, n)
+            slot = (which * 2 + h) * n
+            for i in range(2):
+                into = incoming[which][i].at[it, h, peer]
+                remote(
+                    into, into, st_send.at[it, i, slot + peer], st_recv.at[it, i, slot + peer],
+                    {name: peer},
+                ).wait_recv()
+
+    def total_of(it, which, h):
+        n = ring(which, h)[0]
+        levels, lines = incoming[which]
+        total = decode(levels[it, h, 0], lines[it, h, 0])
+        for p in range(1, n):
+            total = total + decode(levels[it, h, p], lines[it, h, p])
+        value, top = encode(total)
+        levels, lines = outgoing[which + 1]
+        levels[it, h] = value.astype(jnp.int16)
+        lines[it, h] = column_to_line(top)
+
+    def split_images(slot, h, to):
+        together = max(1, 16 // kept)
+        for g in range(0, n_y, together):
+            values = [decode(img_q[slot, h, g + i], img_s[slot, h, g + i]) for i in range(together)]
+            for b in range(2):
+                part = [v[b * kept : (b + 1) * kept] for v in values]
+                high, low = split2(jnp.concatenate(part, axis=0) if together > 1 else part[0])
+                cols = slice(h * half + b * quarter, h * half + (b + 1) * quarter)
+                split[to, g * kept : (g + together) * kept, cols] = high
+                split[to, size + g * kept : size + (g + together) * kept, cols] = low
 
     pending = []
-    eye_low = None
     for it in range(ITERS):
         last = it == ITERS - 1
         left_own = omega_ref[...] if it == 0 else cpl_own[it]
         if it > 0:
             remote(cpl_own.at[it], cpl_far.at[it], c_send.at[it], c_recv.at[it], other).wait_recv()
         left_far = cpl_far[it]
-        flights = []
-        width = min(256, half)
         for h in range(2):
-            for j in range(half // width):
-                cols = slice(h * half + j * width, h * half + (j + 1) * width)
+            for b in range(2):
+                cols = slice(h * half + b * quarter, h * half + (b + 1) * quarter)
                 total = dot_nn(left_own, a_ref[0:points, cols]) + dot_nn(
                     left_far, a_ref[points : 2 * points, cols]
                 )
-                part[it, h, :, :, j * width : (j + 1) * width] = total.reshape(
-                    count[h], size // count[h], width
-                )
-            flights.append(stage(it, 0, h))
-        second = []
+                value, top = encode(total)
+                level[:, b * kept : (b + 1) * kept, :] = value.reshape(n_y, kept, quarter)
+                level_top[:, b * kept : (b + 1) * kept, :] = jnp.broadcast_to(
+                    top, (size, LANES)
+                ).reshape(n_y, kept, LANES)
+            for g in range(n_y):
+                part_q[it, h, g] = level[g].astype(jnp.int16)
+                part_s[it, h, g] = column_to_line(level_top[g][:, 0:1])
+            stage(it, 0, h)
         for h in range(2):
-            me, n = mine[h], count[h]
-            got1[it, h, me] = part[it, h, me]
-            arrive(it, 0, h, flights[h])
-            total = got1[it, h, 0]
-            for p in range(1, n):
-                total = total + got1[it, h, p]
-            sum1[it, h] = total
-            second.append(stage(it, 1, h))
-            got2[it, h, mine[1 - h]] = total
-        third = []
+            arrive(it, 0, h)
+            total_of(it, 0, h)
+            stage(it, 1, h)
         for h in range(2):
-            n = count[1 - h]
-            arrive(it, 1, h, second[h])
-            total = got2[it, h, 0]
-            for p in range(1, n):
-                total = total + got2[it, h, p]
-            sum2[it, h] = total
-            third.append(stage(it, 2, h))
-            img[it, h, mine[h]] = total
+            arrive(it, 1, h)
+            total_of(it, 1, h)
+            stage(it, 2, h)
         for h in range(2):
-            arrive(it, 2, h, third[h])
-            high, low = split2(img[it, h].reshape(size, half))
-            split[0:size, h * half : (h + 1) * half] = high
-            split[size : 2 * size, h * half : (h + 1) * half] = low
+            arrive(it, 2, h)
+            split_images(it, h, 0)
         if last:
-            final = remote(img.at[it], img.at[it + 1], f_send.at[0], f_recv.at[0], other)
-            final.start()
-        both = split[...]
+            final = [
+                remote(img_q.at[it], img_q.at[it + 1], f_send.at[0], f_recv.at[0], other),
+                remote(img_s.at[it], img_s.at[it + 1], f_send.at[1], f_recv.at[1], other),
+            ]
+            for copy in final:
+                copy.start()
+        both = split[0]
         square = dot_nt(both, both)
         square = square[:size] + square[size:]
         square = square + pltpu.roll(square, size, 1)
@@ -308,6 +381,12 @@
                 )
                 copy.start()
                 pending.append(copy)
+        else:
+            for copy in final:
+                copy.wait_recv()
+            pending.extend(final)
+            for h in range(2):
+                split_images(it + 1, h, 1)
         for dx, dc in group:
             peer_x, peer_c = group_peer(dx, dc)
             slot = peer_x * n_c + peer_c
@@ -329,22 +408,23 @@
             total = w_in[it, 0]
             for p in range(1, n_x):
                 total = total + w_in[it, p]
-            cpl_own[it + 1] = apply_factor(inv_high, inv_low, total).astype(jnp.bfloat16)
+            high, low = split2(total)
+            cpl_own[it + 1] = apply_factor(inv_high, inv_low, high, low).astype(jnp.bfloat16)
             copy = remote(
                 cpl_own.at[it + 1], cpl_far.at[it + 1], c_send.at[it + 1], c_recv.at[it + 1], other
             )
             copy.start()
             pending.append(copy)
         else:
-            final.wait()
             width = min(256, half)
             for c in range(2):
-                slot = it + jnp.where(my_c == c, 0, 1)
-                for h in range(2):
-                    for j in range(half // width):
-                        value = img[slot, h, :, :, j * width : (j + 1) * width].reshape(size, width)
-                        start = (c * 2 + h) * half + j * width
-                        out_ref[:, start : start + width] = apply_factor(inv_high, inv_low, value)
+                slot = jnp.where(my_c == c, 0, 1)
+                for j in range(2 * half // width):
+                    cols = slice(j * width, (j + 1) * width)
+                    start = c * 2 * half + j * width
+                    out_ref[:, start : start + width] = apply_factor(
+                        inv_high, inv_low, split[slot, 0:size, cols], split[slot, size : 2 * size, cols]
+                    )
     for copy in pending:
         copy.wait_send()
 
@@ -356,27 +436,30 @@
     n_x = lax.axis_size("freq")
     rows = G // (n_x * n_c)
     freqs = rows * G
-    half = freqs // 2
-    ky, kz = size // n_y, size // n_z
     assert n_y == n_z and n_c == 2
-    f32, bf16, i32 = jnp.float32, jnp.bfloat16, jnp.int32
+    tall, quarter = 2 * (size // n_y), freqs // 4
+    f32, bf16, i32, i16 = jnp.float32, jnp.bfloat16, jnp.int32, jnp.int16
     vmem = pltpu.VMEM
     dma = pltpu.SemaphoreType.DMA
+
+    def blocks(*lead):
+        return [vmem((*lead, tall, quarter), i16), vmem((*lead, 1, LANES), f32)]
+
     scratch = [
         vmem((points, PB * PB), bf16), vmem((1, points), i32), vmem((2, points), i32),
         vmem((3, points, LANES), i32),
         vmem((2 * points, freqs), bf16),
         vmem((ITERS, size, points), bf16), vmem((ITERS, size, points), bf16),
-        vmem((ITERS, 2, n_y, ky, half), f32), vmem((ITERS, 2, n_y, ky, half), f32),
-        vmem((ITERS, 2, ky, half), f32), vmem((ITERS, 2, n_z, ky, half), f32),
-        vmem((ITERS, 2, ky, half), f32), vmem((ITERS + 1, 2, n_y, ky, half), f32),
-        vmem((2 * size, freqs), bf16),
+        vmem((n_y, tall, quarter), i32), vmem((n_y, tall, LANES), f32),
+        *blocks(ITERS, 2, n_y), *blocks(ITERS, 2, n_y), *blocks(ITERS, 2), *blocks(ITERS, 2, n_z),
+        *blocks(ITERS, 2), *blocks(ITERS + 1, 2, n_y),
+        vmem((2, 2 * size, freqs), bf16),
         vmem((ITERS, size // 2, LANES), f32), vmem((ITERS, n_x * n_c, size // 2, LANES), f32),
         vmem((ITERS, size, points), f32), vmem((ITERS, size, points), f32),
         vmem((ITERS, size, points), f32), vmem((ITERS, n_x, size, points), f32),
-        dma((4,)), dma((4,)), dma((ITERS, 6 * n_y)), dma((ITERS, 6 * n_y)),
+        dma((4,)), dma((4,)), dma((ITERS, 2, 6 * n_y)), dma((ITERS, 2, 6 * n_y)),
         dma((ITERS, n_x * n_c)), dma((ITERS, n_x * n_c)), dma((ITERS,)), dma((ITERS,)),
-        dma((ITERS, n_x)), dma((ITERS, n_x)), dma((ITERS,)), dma((ITERS,)), dma((1,)), dma((1,)),
+        dma((ITERS, n_x)), dma((ITERS, n_x)), dma((ITERS,)), dma((ITERS,)), dma((2,)), dma((2,)),
     ]
     out = pl.pallas_call(
         functools.partial(kernel, (n_y, n_z, n_c, n_x)),

time: 154 us -> 112 us (0.73)
  Pallas kernels: 151 us -> 109 us
    pallas_call x1, Pallas kernels: 151 us -> 109 us  [shards(): pl.pallas_call(functools.partial(kernel, (n_y, n_z, n_c, n_x)), out_shape...]
where the time goes in v1:
time: 112 us
  Pallas kernels  109 us (97%)
  local copies, waits for them, and re-layouts  2.27 us (2%)
    pallas_call x1, Pallas kernels, shards(): pl.pallas_call(functools.partial(kernel, (n_y, n_z, n_c, n_x)), out_shape...  109 us
    unnamed x1, local copies, waits for them, and re-layouts  2.27 us

profile of v1, /device:TPU:1, one launch (start us, length us, event | category | flops | bytes accessed | tf_op | source)
XLA Modules:
  0.0 111.8 jit_solution(15347823230188662431)
XLA Ops:
  0.0 109.5 %shard_map.46 = f32[64,4096]{1,0:T(8,128)} custom-call(bf16[256,1024]{1,0:T(8,128)(2,1)} %pupil_ref.1, s32[1,256]{1,0:T(1,128)} %bitcast.5, s32[2,256]{1,0:T(2,128)} %off_ref.1, bf16[64,256]{1,0:T(8,128)(2,1)} %bitcast.4), custom_call_target="tpu_custom_call" | custom-call | tf_op jit(solution)/shard_map/pallas_call | solution.py:464
  109.5 2.3 %copy.6 = f32[4096,64]{0,1:T(8,128)} copy(f32[4096,64]{0,1:T(8,128)} %bitcast.3) | data formatting | bytes 2097152

commit v2 on v1

--- a/solution.py
+++ b/solution.py
@@ -181,20 +181,20 @@
 
 
 def kernel(
-    sizes, pupil_ref, on_ref, off_ref, omega_ref, out_ref,
-    pupil_far, on_far, off_far, meta, a_ref, cpl_own, cpl_far,
+    sizes, pupil_hbm, on_hbm, off_hbm, omega_hbm, out_ref,
+    pupil_ref, on_ref, off_ref, omega_ref, pupil_far, on_far, off_far, meta, a_ref, cpl_own, cpl_far,
     level, level_top, part_q, part_s, got1_q, got1_s, sum1_q, sum1_s, got2_q, got2_s, sum2_q, sum2_s,
-    img_q, img_s, split, gram_out, gram_in, w_far, w_far_in, w_own, w_in,
+    img_q, img_s, split, gram_out, gram_in, w_far, w_far_in, w_q, w_s, w_in_q, w_in_s,
     setup_send, setup_recv, st_send, st_recv, gram_send, gram_recv, w_send, w_recv, x_send, x_recv,
-    c_send, c_recv, f_send, f_recv,
+    c_send, c_recv, f_send, f_recv, load_sem,
 ):
     n_y, n_z, n_c, n_x = sizes
     my_y, my_z = lax.axis_index("src_0"), lax.axis_index("src_1")
     my_c, my_x = lax.axis_index("src_2"), lax.axis_index("freq")
     other = {"src_2": 1 - my_c}
     rows = G // (n_x * n_c)
-    size = omega_ref.shape[0]
-    points = pupil_ref.shape[0]
+    size = omega_hbm.shape[0]
+    points = pupil_hbm.shape[0]
     half = rows * G // 2
     quarter = half // 2
     axes = ("src_0", "src_1")
@@ -224,6 +224,14 @@
         pl.semaphore_signal(
             barrier, inc=1, device_id={"freq": peer_x, "src_2": peer_c}, device_id_type=MESH_ID
         )
+    local = [
+        pltpu.make_async_copy(src, dst, load_sem.at[i])
+        for i, (src, dst) in enumerate(
+            ((off_hbm, off_ref), (on_hbm, on_ref), (omega_hbm, omega_ref), (pupil_hbm, pupil_ref))
+        )
+    ]
+    for copy in local:
+        copy.start()
     pl.semaphore_wait(barrier, n_y - 1 + n_z - 1 + len(group))
 
     def remote(src, dst, send, recv, device):
@@ -235,11 +243,13 @@
     setup = [
         remote(src, dst, setup_send.at[i], setup_recv.at[i], other)
         for i, (src, dst) in enumerate(
-            ((off_ref, off_far), (on_ref, on_far), (omega_ref, cpl_far.at[0]), (pupil_ref, pupil_far))
+            ((off_hbm, off_far), (on_hbm, on_far), (omega_hbm, cpl_far.at[0]), (pupil_hbm, pupil_far))
         )
     ]
     for copy in setup:
         copy.start()
+    for copy in local:
+        copy.wait()
     base_row = my_x * (rows * n_c) + my_c * rows
     place_windows(pupil_ref, off_ref, on_ref, meta, a_ref, 0, base_row, rows)
     for copy in setup:
@@ -371,16 +381,20 @@
             own = own[:size] + own[size:]
             swap.wait_recv()
             own = own + w_far_in[it]
-            w_own[it] = own
-            w_in[it, my_x] = own
+            value, top = encode(own)
+            w_q[it] = value.astype(jnp.int16)
+            w_s[it] = column_to_line(top)
             for d in offsets_far_first(n_x):
                 peer = lax.rem(my_x + d, n_x)
-                copy = remote(
-                    w_own.at[it], w_in.at[it, my_x], x_send.at[it, d], x_recv.at[it, my_x],
-                    {"freq": peer},
-                )
-                copy.start()
-                pending.append(copy)
+                for i, (src, dst) in enumerate(((w_q, w_in_q), (w_s, w_in_s))):
+                    copy = remote(
+                        src.at[it], dst.at[it, my_x], x_send.at[it, i, d], x_recv.at[it, i, my_x],
+                        {"freq": peer},
+                    )
+                    copy.start()
+                    pending.append(copy)
+            w_in_q[it, my_x] = w_q[it]
+            w_in_s[it, my_x] = w_s[it]
         else:
             for copy in final:
                 copy.wait_recv()
@@ -401,13 +415,14 @@
         if not last:
             for d in offsets_far_first(n_x):
                 peer = lax.rem(my_x + d, n_x)
-                remote(
-                    w_own.at[it], w_in.at[it, peer], x_send.at[it, d], x_recv.at[it, peer],
-                    {"freq": peer},
-                ).wait_recv()
-            total = w_in[it, 0]
+                for i, dst in enumerate((w_in_q, w_in_s)):
+                    remote(
+                        dst.at[it, peer], dst.at[it, peer], x_send.at[it, i, d],
+                        x_recv.at[it, i, peer], {"freq": peer},
+                    ).wait_recv()
+            total = decode(w_in_q[it, 0], w_in_s[it, 0])
             for p in range(1, n_x):
-                total = total + w_in[it, p]
+                total = total + decode(w_in_q[it, p], w_in_s[it, p])
             high, low = split2(total)
             cpl_own[it + 1] = apply_factor(inv_high, inv_low, high, low).astype(jnp.bfloat16)
             copy = remote(
@@ -447,6 +462,8 @@
 
     scratch = [
         vmem((points, PB * PB), bf16), vmem((1, points), i32), vmem((2, points), i32),
+        vmem((size, points), bf16),
+        vmem((points, PB * PB), bf16), vmem((1, points), i32), vmem((2, points), i32),
         vmem((3, points, LANES), i32),
         vmem((2 * points, freqs), bf16),
         vmem((ITERS, size, points), bf16), vmem((ITERS, size, points), bf16),
@@ -456,19 +473,21 @@
         vmem((2, 2 * size, freqs), bf16),
         vmem((ITERS, size // 2, LANES), f32), vmem((ITERS, n_x * n_c, size // 2, LANES), f32),
         vmem((ITERS, size, points), f32), vmem((ITERS, size, points), f32),
-        vmem((ITERS, size, points), f32), vmem((ITERS, n_x, size, points), f32),
+        vmem((ITERS, size, points), i16), vmem((ITERS, 1, LANES), f32),
+        vmem((ITERS, n_x, size, points), i16), vmem((ITERS, n_x, 1, LANES), f32),
         dma((4,)), dma((4,)), dma((ITERS, 2, 6 * n_y)), dma((ITERS, 2, 6 * n_y)),
         dma((ITERS, n_x * n_c)), dma((ITERS, n_x * n_c)), dma((ITERS,)), dma((ITERS,)),
-        dma((ITERS, n_x)), dma((ITERS, n_x)), dma((ITERS,)), dma((ITERS,)), dma((2,)), dma((2,)),
+        dma((ITERS, 2, n_x)), dma((ITERS, 2, n_x)), dma((ITERS,)), dma((ITERS,)), dma((2,)), dma((2,)),
+        dma((4,)),
     ]
     out = pl.pallas_call(
         functools.partial(kernel, (n_y, n_z, n_c, n_x)),
         out_shape=jax.ShapeDtypeStruct((size, freqs * n_c), f32),
-        in_specs=[pl.BlockSpec(memory_space=pltpu.VMEM)] * 4,
+        in_specs=[pl.BlockSpec(memory_space=pltpu.HBM)] * 4,
         out_specs=pl.BlockSpec(memory_space=pltpu.VMEM),
         scratch_shapes=scratch,
         compiler_params=pltpu.CompilerParams(
-            collective_id=0, has_side_effects=True, vmem_limit_bytes=60 * 1024 * 1024
+            collective_id=0, has_side_effects=True, vmem_limit_bytes=14 * 1024 * 1024
         ),
     )(pupil_block, source_on.reshape(1, points), offsets, omega.T)
     return out.T

time: 112 us -> 111 us (level)
  Pallas kernels: 109 us -> 107 us
  local copies, waits for them, and re-layouts: 2.27 us -> 3.46 us
    pallas_call x1, Pallas kernels: 109 us -> 107 us  [shards(): pl.pallas_call(functools.partial(kernel, (n_y, n_z, n_c, n_x)), out_shape...]
    unnamed x1 -> x9, local copies, waits for them, and re-layouts: 2.27 us -> 3.46 us
where the time goes in v2:
time: 111 us
  Pallas kernels  107 us (96%)
  local copies, waits for them, and re-layouts  3.46 us (3%)
    pallas_call x1, Pallas kernels, shards(): pl.pallas_call(functools.partial(kernel, (n_y, n_z, n_c, n_x)), out_shape...  107 us
    unnamed x9, local copies, waits for them, and re-layouts  3.46 us

profile of v2, /device:TPU:1, one launch (start us, length us, event | category | flops | bytes accessed | tf_op | source)
XLA Modules:
  0.0 110.9 jit_solution(7569218630773015030)
XLA Ops:
  0.0 0.0 copy-start.2
  0.0 0.0 copy-start.3
  0.0 0.7 copy-done.2
  0.7 0.0 copy-done.3
  0.7 0.0 copy-start
  0.7 1.0 copy-done
  1.7 0.0 copy-start.1
  1.7 0.8 copy-done.1
  2.5 107.4 %shard_map.46 = f32[64,4096]{1,0:T(8,128)S(1)} custom-call(bf16[256,1024]{1,0:T(8,128)(2,1)S(1)} %copy-done, s32[1,256]{1,0:T(1,128)S(1)} %bitcast.5, s32[2,256]{1,0:T(2,128)S(1)} %copy-done.2, bf16[64,256]{1,0:T(8,128)(2,1)S(1)} %bitcast.4), custom_call_target="tpu_custom_call" | custom-call | tf_op jit(solution)/shard_map/pallas_call | solution.py:483
  109.9 1.0 copy.6
Async XLA Ops:
  0.0 0.7 copy-start.2
  0.0 0.7 copy-start.3
  0.7 1.0 copy-start
  1.7 0.8 copy-start.1

commit v3 on v2

--- a/solution.py
+++ b/solution.py
@@ -64,11 +64,7 @@
     return level.astype(jnp.int32).astype(jnp.float32) * (top * (1.0 / LEVELS))
 
 
-def place_windows(pupil_ref, off_ref, on_ref, meta_ref, a_ref, a_row, base_row, rows):
-    points = pupil_ref.shape[0]
-    per = LANES // PB
-    chunk = min(64, points)
-
+def spread_meta(off_ref, on_ref, meta_ref, points):
     def spread(line):
         return jnp.transpose(jnp.broadcast_to(line, (LANES, points)))
 
@@ -76,8 +72,13 @@
     meta_ref[1] = spread(off_ref[1:2, :])
     meta_ref[2] = spread(on_ref[0:1, :])
 
+
+def place_windows(pupil_ref, meta_ref, a_ref, a_row, first, points, base_row, rows):
+    per = LANES // PB
+    chunk = min(64, points)
+
     def block(index, carry):
-        s0 = pl.multiple_of(index * chunk, chunk)
+        s0 = pl.multiple_of(first + index * chunk, chunk)
         row_off = meta_ref[0, pl.ds(s0, chunk), :]
         col_off = meta_ref[1, pl.ds(s0, chunk), :]
         lit = meta_ref[2, pl.ds(s0, chunk), :].astype(jnp.float32)
@@ -131,10 +132,22 @@
     full = (8, LANES)
     lane = lax.broadcasted_iota(jnp.int32, full, 1)
     sub = lax.broadcasted_iota(jnp.int32, full, 0)
+    unit = jnp.broadcast_to(jnp.broadcast_to(packed[0:8, 0:1], full)[0:1, :], full)
+    per_unit = 1.0 / unit
     tiles = []
     for t in range(size // 8):
         eye = jnp.where(lane == sub + 8 * t, 1.0, 0.0)
-        tiles.append(jnp.where(lane < size, eye, whole[8 * t : 8 * t + 8]))
+        tiles.append(jnp.where(lane < size, eye, whole[8 * t : 8 * t + 8] * per_unit))
+
+    def pair(block, k):
+        a, b, d = block[k][k], block[k + 1][k], block[k + 1][k + 1]
+        per = 1.0 / (a * d - b * b)
+        return (d * per, b * per, a * per), b * (1.0 / a)
+
+    def through(inverse, first, second):
+        p, q, r = inverse
+        return p * first - q * second, r * second - q * first
+
     wide = 4
     for k in range(0, size, wide):
         home, first = k // 8, k % 8
@@ -147,26 +160,24 @@
             [jnp.broadcast_to(columns[0][j][first + i : first + i + 1, :], full) for j in range(i + 1)]
             for i in range(wide)
         ]
-        ratio, scaled = {}, []
-        for p in range(wide):
-            inverse = 1.0 / block[p][p]
-            for i in range(p + 1, wide):
-                ratio[i, p] = block[i][p] * inverse
-                for j in range(p + 1, i + 1):
-                    block[i][j] = block[i][j] - ratio[i, p] * block[j][p]
-            for i in range(p + 1, wide):
-                lines[i] = lines[i] - ratio[i, p] * lines[p]
-            scaled.append(lines[p] * inverse)
+        inverse, ratio = pair(block, 0)
+        upper = through(inverse, lines[0], lines[1])
+        weights = {}
+        for i in (2, 3):
+            weights[i] = through(inverse, block[i][0], block[i][1])
+            for j in range(2, i + 1):
+                block[i][j] = block[i][j] - (weights[i][0] * block[j][0] + weights[i][1] * block[j][1])
+            lines[i] = lines[i] - (weights[i][0] * lines[0] + weights[i][1] * lines[1])
+        lines[1] = lines[1] - ratio * lines[0]
+        inverse, ratio = pair(block, 2)
+        lower = through(inverse, lines[2], lines[3])
+        lines[3] = lines[3] - ratio * lines[2]
         for t in range(home, size // 8):
             own = columns[t - home]
-            taken = None
-            for p in range(wide):
-                weight = own[p]
-                for q in range(p):
-                    weight = weight - ratio[p, q] * own[q]
-                own[p] = weight
-                term = weight * scaled[p]
-                taken = term if taken is None else taken + term
+            third, fourth = (
+                own[i] - (own[0] * weights[i][0] + own[1] * weights[i][1]) for i in (2, 3)
+            )
+            taken = (own[0] * upper[0] + own[1] * upper[1]) + (third * lower[0] + fourth * lower[1])
             updated = tiles[t] - taken
             if t == home:
                 updated = jnp.where(sub >= first + wide, updated, tiles[t])
@@ -176,7 +187,7 @@
     done = []
     for t in range(size // 8):
         pivot = jnp.sum(jnp.where(lane == sub + (8 * t + size), tiles[t], 0.0), axis=1, keepdims=True)
-        done.append(tiles[t] * lax.rsqrt(pivot))
+        done.append(tiles[t] * lax.rsqrt(pivot * unit[:, 0:1]))
     return jnp.concatenate(done, axis=0)[:, :size]
 
 
@@ -205,7 +216,10 @@
     def offsets_far_first(n):
         return sorted(range(1, n), key=lambda d: (-min(d, n - d), d))
 
-    group = [(dx, dc) for dx in range(n_x) for dc in range(n_c) if dx or dc]
+    group = sorted(
+        ((dx, dc) for dx in range(n_x) for dc in range(n_c) if dx or dc),
+        key=lambda step: -min(step[0], n_x - step[0]),
+    )
 
     def group_peer(dx, dc):
         peer_x = lax.rem(my_x + dx, n_x)
@@ -240,10 +254,12 @@
             device_id=device, device_id_type=MESH_ID,
         )
 
+    parts = [pl.ds(0, points // 2), pl.ds(points // 2, points // 2)]
     setup = [
         remote(src, dst, setup_send.at[i], setup_recv.at[i], other)
         for i, (src, dst) in enumerate(
-            ((off_hbm, off_far), (on_hbm, on_far), (omega_hbm, cpl_far.at[0]), (pupil_hbm, pupil_far))
+            ((off_hbm, off_far), (on_hbm, on_far), (omega_hbm, cpl_far.at[0]),
+             *((pupil_hbm.at[part], pupil_far.at[part]) for part in parts))
         )
     ]
     for copy in setup:
@@ -251,10 +267,15 @@
     for copy in local:
         copy.wait()
     base_row = my_x * (rows * n_c) + my_c * rows
-    place_windows(pupil_ref, off_ref, on_ref, meta, a_ref, 0, base_row, rows)
-    for copy in setup:
-        copy.wait()
-    place_windows(pupil_far, off_far, on_far, meta, a_ref, points, base_row, rows)
+    spread_meta(off_ref, on_ref, meta, points)
+    place_windows(pupil_ref, meta, a_ref, 0, 0, points, base_row, rows)
+    for copy in setup[:-1]:
+        copy.wait_recv()
+    spread_meta(off_far, on_far, meta, points)
+    place_windows(pupil_far, meta, a_ref, points, 0, points // 2, base_row, rows)
+    setup[-1].wait_recv()
+    place_windows(pupil_far, meta, a_ref, points, points // 2, points // 2, base_row, rows)
+    pending = list(setup)
 
     outgoing = ((part_q, part_s), (sum1_q, sum1_s), (sum2_q, sum2_s))
     incoming = ((got1_q, got1_s), (got2_q, got2_s), (img_q, img_s))
@@ -280,41 +301,60 @@
             src = outgoing[which][i].at[it, h]
             incoming[which][i][it, h, me] = src[me] if which == 0 else src[...]
 
-    def arrive(it, which, h):
+    def arrive(it, which, h, peer):
         n, me, name = ring(which, h)
-        for d in offsets_far_first(n):
-            peer = lax.rem(me + d, n)
-            slot = (which * 2 + h) * n
-            for i in range(2):
-                into = incoming[which][i].at[it, h, peer]
-                remote(
-                    into, into, st_send.at[it, i, slot + peer], st_recv.at[it, i, slot + peer],
-                    {name: peer},
-                ).wait_recv()
+        slot = (which * 2 + h) * n
+        for i in range(2):
+            into = incoming[which][i].at[it, h, peer]
+            remote(
+                into, into, st_send.at[it, i, slot + peer], st_recv.at[it, i, slot + peer],
+                {name: peer},
+            ).wait_recv()
 
     def total_of(it, which, h):
-        n = ring(which, h)[0]
+        n, me, name = ring(which, h)
         levels, lines = incoming[which]
-        total = decode(levels[it, h, 0], lines[it, h, 0])
-        for p in range(1, n):
-            total = total + decode(levels[it, h, p], lines[it, h, p])
+        if which == 0:
+            total = decode(levels[it, h, me], lines[it, h, me])
+            for d in offsets_far_first(n):
+                peer = lax.rem(me + d, n)
+                arrive(it, which, h, peer)
+                total = total + decode(levels[it, h, peer], lines[it, h, peer])
+        else:
+            for d in offsets_far_first(n):
+                arrive(it, which, h, lax.rem(me + d, n))
+            total = decode(levels[it, h, 0], lines[it, h, 0])
+            for p in range(1, n):
+                total = total + decode(levels[it, h, p], lines[it, h, p])
         value, top = encode(total)
         levels, lines = outgoing[which + 1]
         levels[it, h] = value.astype(jnp.int16)
         lines[it, h] = column_to_line(top)
 
-    def split_images(slot, h, to):
+    def split_images(slot, h, to, waits):
         together = max(1, 16 // kept)
-        for g in range(0, n_y, together):
+        n, me, name = ring(2, h)
+        teams = n // together
+        for step in range(teams):
+            if waits:
+                g = lax.rem(me // together + step, teams) * together
+                for i in range(together):
+                    if step:
+                        arrive(slot, 2, h, g + i)
+                    else:
+                        for d in range(1, together):
+                            arrive(slot, 2, h, g + lax.rem(me + d, together)) if i == 0 else None
+            else:
+                g = step * together
             values = [decode(img_q[slot, h, g + i], img_s[slot, h, g + i]) for i in range(together)]
+            base = pl.multiple_of(g * kept, together * kept) if waits else g * kept
             for b in range(2):
                 part = [v[b * kept : (b + 1) * kept] for v in values]
                 high, low = split2(jnp.concatenate(part, axis=0) if together > 1 else part[0])
                 cols = slice(h * half + b * quarter, h * half + (b + 1) * quarter)
-                split[to, g * kept : (g + together) * kept, cols] = high
-                split[to, size + g * kept : size + (g + together) * kept, cols] = low
-
-    pending = []
+                split[to, pl.ds(base, together * kept), cols] = high
+                split[to, pl.ds(size + base, together * kept), cols] = low
+
     for it in range(ITERS):
         last = it == ITERS - 1
         left_own = omega_ref[...] if it == 0 else cpl_own[it]
@@ -337,16 +377,13 @@
                 part_s[it, h, g] = column_to_line(level_top[g][:, 0:1])
             stage(it, 0, h)
         for h in range(2):
-            arrive(it, 0, h)
             total_of(it, 0, h)
             stage(it, 1, h)
         for h in range(2):
-            arrive(it, 1, h)
             total_of(it, 1, h)
             stage(it, 2, h)
         for h in range(2):
-            arrive(it, 2, h)
-            split_images(it, h, 0)
+            split_images(it, h, 0, True)
         if last:
             final = [
                 remote(img_q.at[it], img_q.at[it + 1], f_send.at[0], f_recv.at[0], other),
@@ -400,7 +437,7 @@
                 copy.wait_recv()
             pending.extend(final)
             for h in range(2):
-                split_images(it + 1, h, 1)
+                split_images(it + 1, h, 1, False)
         for dx, dc in group:
             peer_x, peer_c = group_peer(dx, dc)
             slot = peer_x * n_c + peer_c
@@ -475,7 +512,7 @@
         vmem((ITERS, size, points), f32), vmem((ITERS, size, points), f32),
         vmem((ITERS, size, points), i16), vmem((ITERS, 1, LANES), f32),
         vmem((ITERS, n_x, size, points), i16), vmem((ITERS, n_x, 1, LANES), f32),
-        dma((4,)), dma((4,)), dma((ITERS, 2, 6 * n_y)), dma((ITERS, 2, 6 * n_y)),
+        dma((5,)), dma((5,)), dma((ITERS, 2, 6 * n_y)), dma((ITERS, 2, 6 * n_y)),
         dma((ITERS, n_x * n_c)), dma((ITERS, n_x * n_c)), dma((ITERS,)), dma((ITERS,)),
         dma((ITERS, 2, n_x)), dma((ITERS, 2, n_x)), dma((ITERS,)), dma((ITERS,)), dma((2,)), dma((2,)),
         dma((4,)),
@@ -489,7 +526,12 @@
         compiler_params=pltpu.CompilerParams(
             collective_id=0, has_side_effects=True, vmem_limit_bytes=14 * 1024 * 1024
         ),
-    )(pupil_block, source_on.reshape(1, points), offsets, omega.T)
+    )(
+        *(
+            pltpu.with_memory_space_constraint(value, pltpu.HBM)
+            for value in (pupil_block, source_on.reshape(1, points), offsets, omega.T)
+        )
+    )
     return out.T
 
 

time: 111 us -> 109 us (0.982)
  local copies, waits for them, and re-layouts: 3.46 us -> 0.97 us
    unnamed x9 -> x1, local copies, waits for them, and re-layouts: 3.46 us -> 0.97 us
where the time goes in v3:
time: 109 us
  Pallas kernels  108 us (99%)
    pallas_call x1, Pallas kernels, shards(): pl.pallas_call(functools.partial(kernel, (n_y, n_z, n_c, n_x)), out_shape...  108 us

profile of v3, /device:TPU:1, one launch (start us, length us, event | category | flops | bytes accessed | tf_op | source)
XLA Modules:
  0.0 109.2 jit_solution(17558323827470080753)
XLA Ops:
  0.0 108.2 %shard_map.46 = f32[64,4096]{1,0:T(8,128)S(1)} custom-call(bf16[256,1024]{1,0:T(8,128)(2,1)} %pupil_hbm.1, s32[1,256]{1,0:T(1,128)} %bitcast.5, s32[2,256]{1,0:T(2,128)} %off_hbm.1, bf16[64,256]{1,0:T(8,128)(2,1)} %bitcast.4), custom_call_target="tpu_custom_call" | custom-call | tf_op jit(solution)/shard_map/pallas_call | solution.py:520
  108.3 1.0 copy.6

commit v4 on v3

--- a/solution.py
+++ b/solution.py
@@ -301,59 +301,39 @@
             src = outgoing[which][i].at[it, h]
             incoming[which][i][it, h, me] = src[me] if which == 0 else src[...]
 
-    def arrive(it, which, h, peer):
+    def arrive(it, which, h):
         n, me, name = ring(which, h)
-        slot = (which * 2 + h) * n
-        for i in range(2):
-            into = incoming[which][i].at[it, h, peer]
-            remote(
-                into, into, st_send.at[it, i, slot + peer], st_recv.at[it, i, slot + peer],
-                {name: peer},
-            ).wait_recv()
+        for d in offsets_far_first(n):
+            peer = lax.rem(me + d, n)
+            slot = (which * 2 + h) * n
+            for i in range(2):
+                into = incoming[which][i].at[it, h, peer]
+                remote(
+                    into, into, st_send.at[it, i, slot + peer], st_recv.at[it, i, slot + peer],
+                    {name: peer},
+                ).wait_recv()
 
     def total_of(it, which, h):
-        n, me, name = ring(which, h)
+        n = ring(which, h)[0]
         levels, lines = incoming[which]
-        if which == 0:
-            total = decode(levels[it, h, me], lines[it, h, me])
-            for d in offsets_far_first(n):
-                peer = lax.rem(me + d, n)
-                arrive(it, which, h, peer)
-                total = total + decode(levels[it, h, peer], lines[it, h, peer])
-        else:
-            for d in offsets_far_first(n):
-                arrive(it, which, h, lax.rem(me + d, n))
-            total = decode(levels[it, h, 0], lines[it, h, 0])
-            for p in range(1, n):
-                total = total + decode(levels[it, h, p], lines[it, h, p])
+        total = decode(levels[it, h, 0], lines[it, h, 0])
+        for p in range(1, n):
+            total = total + decode(levels[it, h, p], lines[it, h, p])
         value, top = encode(total)
         levels, lines = outgoing[which + 1]
         levels[it, h] = value.astype(jnp.int16)
         lines[it, h] = column_to_line(top)
 
-    def split_images(slot, h, to, waits):
+    def split_images(slot, h, to):
         together = max(1, 16 // kept)
-        n, me, name = ring(2, h)
-        teams = n // together
-        for step in range(teams):
-            if waits:
-                g = lax.rem(me // together + step, teams) * together
-                for i in range(together):
-                    if step:
-                        arrive(slot, 2, h, g + i)
-                    else:
-                        for d in range(1, together):
-                            arrive(slot, 2, h, g + lax.rem(me + d, together)) if i == 0 else None
-            else:
-                g = step * together
+        for g in range(0, n_y, together):
             values = [decode(img_q[slot, h, g + i], img_s[slot, h, g + i]) for i in range(together)]
-            base = pl.multiple_of(g * kept, together * kept) if waits else g * kept
             for b in range(2):
                 part = [v[b * kept : (b + 1) * kept] for v in values]
                 high, low = split2(jnp.concatenate(part, axis=0) if together > 1 else part[0])
                 cols = slice(h * half + b * quarter, h * half + (b + 1) * quarter)
-                split[to, pl.ds(base, together * kept), cols] = high
-                split[to, pl.ds(size + base, together * kept), cols] = low
+                split[to, g * kept : (g + together) * kept, cols] = high
+                split[to, size + g * kept : size + (g + together) * kept, cols] = low
 
     for it in range(ITERS):
         last = it == ITERS - 1
@@ -377,13 +357,16 @@
                 part_s[it, h, g] = column_to_line(level_top[g][:, 0:1])
             stage(it, 0, h)
         for h in range(2):
+            arrive(it, 0, h)
             total_of(it, 0, h)
             stage(it, 1, h)
         for h in range(2):
+            arrive(it, 1, h)
             total_of(it, 1, h)
             stage(it, 2, h)
         for h in range(2):
-            split_images(it, h, 0, True)
+            arrive(it, 2, h)
+            split_images(it, h, 0)
         if last:
             final = [
                 remote(img_q.at[it], img_q.at[it + 1], f_send.at[0], f_recv.at[0], other),
@@ -437,7 +420,7 @@
                 copy.wait_recv()
             pending.extend(final)
             for h in range(2):
-                split_images(it + 1, h, 1, False)
+                split_images(it + 1, h, 1)
         for dx, dc in group:
             peer_x, peer_c = group_peer(dx, dc)
             slot = peer_x * n_c + peer_c

time: 109 us -> 107 us (0.982)
  Pallas kernels: 108 us -> 106 us
    pallas_call x1, Pallas kernels: 108 us -> 106 us  [shards(): pl.pallas_call(functools.partial(kernel, (n_y, n_z, n_c, n_x)), out_shape...]
where the time goes in v4:
time: 107 us
  Pallas kernels  106 us (99%)
    pallas_call x1, Pallas kernels, shards(): pl.pallas_call(functools.partial(kernel, (n_y, n_z, n_c, n_x)), out_shape...  106 us

profile of v4, /device:TPU:1, one launch (start us, length us, event | category | flops | bytes accessed | tf_op | source)
XLA Modules:
  0.0 107.1 jit_solution(2707138533107820359)
XLA Ops:
  0.0 106.1 %shard_map.46 = f32[64,4096]{1,0:T(8,128)S(1)} custom-call(bf16[256,1024]{1,0:T(8,128)(2,1)} %pupil_hbm.1, s32[1,256]{1,0:T(1,128)} %bitcast.5, s32[2,256]{1,0:T(2,128)} %off_hbm.1, bf16[64,256]{1,0:T(8,128)(2,1)} %bitcast.4), custom_call_target="tpu_custom_call" | custom-call | tf_op jit(solution)/shard_map/pallas_call | solution.py:503
  106.1 1.0 copy.6

commit v5 on v4

--- a/solution.py
+++ b/solution.py
@@ -38,6 +38,10 @@
 
 def apply_factor(inv_high, inv_low, high, low):
     return dot_nn(inv_high, high) + (dot_nn(inv_high, low) + dot_nn(inv_low, high))
+
+
+def apply_stacked(inv_twice, inv_low, both):
+    return dot_nn(inv_twice, both) + dot_nn(inv_low, both[: both.shape[0] // 2])
 
 
 def encode(value):
@@ -197,7 +201,7 @@
     level, level_top, part_q, part_s, got1_q, got1_s, sum1_q, sum1_s, got2_q, got2_s, sum2_q, sum2_s,
     img_q, img_s, split, gram_out, gram_in, w_far, w_far_in, w_q, w_s, w_in_q, w_in_s,
     setup_send, setup_recv, st_send, st_recv, gram_send, gram_recv, w_send, w_recv, x_send, x_recv,
-    c_send, c_recv, f_send, f_recv, load_sem,
+    c_send, c_recv, f_send, f_recv, load_sem, own_part,
 ):
     n_y, n_z, n_c, n_x = sizes
     my_y, my_z = lax.axis_index("src_0"), lax.axis_index("src_1")
@@ -284,7 +288,7 @@
         along = h if which != 1 else 1 - h
         return count[along], mine[along], axes[along]
 
-    def stage(it, which, h):
+    def stage(it, which, h, pending):
         n, me, name = ring(which, h)
         for d in offsets_far_first(n):
             peer = lax.rem(me + d, n)
@@ -338,15 +342,19 @@
     for it in range(ITERS):
         last = it == ITERS - 1
         left_own = omega_ref[...] if it == 0 else cpl_own[it]
+        blocks = [
+            slice(h * half + b * quarter, h * half + (b + 1) * quarter) for h in range(2) for b in range(2)
+        ]
         if it > 0:
+            for cols in blocks:
+                own_part[:, cols] = dot_nn(left_own, a_ref[0:points, cols])
             remote(cpl_own.at[it], cpl_far.at[it], c_send.at[it], c_recv.at[it], other).wait_recv()
         left_far = cpl_far[it]
         for h in range(2):
             for b in range(2):
-                cols = slice(h * half + b * quarter, h * half + (b + 1) * quarter)
-                total = dot_nn(left_own, a_ref[0:points, cols]) + dot_nn(
-                    left_far, a_ref[points : 2 * points, cols]
-                )
+                cols = blocks[2 * h + b]
+                near = own_part[:, cols] if it > 0 else dot_nn(left_own, a_ref[0:points, cols])
+                total = near + dot_nn(left_far, a_ref[points : 2 * points, cols])
                 value, top = encode(total)
                 level[:, b * kept : (b + 1) * kept, :] = value.reshape(n_y, kept, quarter)
                 level_top[:, b * kept : (b + 1) * kept, :] = jnp.broadcast_to(
@@ -355,15 +363,15 @@
             for g in range(n_y):
                 part_q[it, h, g] = level[g].astype(jnp.int16)
                 part_s[it, h, g] = column_to_line(level_top[g][:, 0:1])
-            stage(it, 0, h)
+            stage(it, 0, h, pending)
         for h in range(2):
             arrive(it, 0, h)
             total_of(it, 0, h)
-            stage(it, 1, h)
+            stage(it, 1, h, pending)
         for h in range(2):
             arrive(it, 1, h)
             total_of(it, 1, h)
-            stage(it, 2, h)
+            stage(it, 2, h, pending)
         for h in range(2):
             arrive(it, 2, h)
             split_images(it, h, 0)
@@ -374,6 +382,7 @@
             ]
             for copy in final:
                 copy.start()
+        drained, pending = pending, []
         both = split[0]
         square = dot_nt(both, both)
         square = square[:size] + square[size:]
@@ -421,6 +430,8 @@
             pending.extend(final)
             for h in range(2):
                 split_images(it + 1, h, 1)
+        for copy in drained:
+            copy.wait_send()
         for dx, dc in group:
             peer_x, peer_c = group_peer(dx, dc)
             slot = peer_x * n_c + peer_c
@@ -452,13 +463,14 @@
             pending.append(copy)
         else:
             width = min(256, half)
+            inv_twice = jnp.concatenate([inv_high, inv_high], axis=1)
             for c in range(2):
                 slot = jnp.where(my_c == c, 0, 1)
                 for j in range(2 * half // width):
                     cols = slice(j * width, (j + 1) * width)
                     start = c * 2 * half + j * width
-                    out_ref[:, start : start + width] = apply_factor(
-                        inv_high, inv_low, split[slot, 0:size, cols], split[slot, size : 2 * size, cols]
+                    out_ref[:, start : start + width] = apply_stacked(
+                        inv_twice, inv_low, split[slot, :, cols]
                     )
     for copy in pending:
         copy.wait_send()
@@ -498,7 +510,7 @@
         dma((5,)), dma((5,)), dma((ITERS, 2, 6 * n_y)), dma((ITERS, 2, 6 * n_y)),
         dma((ITERS, n_x * n_c)), dma((ITERS, n_x * n_c)), dma((ITERS,)), dma((ITERS,)),
         dma((ITERS, 2, n_x)), dma((ITERS, 2, n_x)), dma((ITERS,)), dma((ITERS,)), dma((2,)), dma((2,)),
-        dma((4,)),
+        dma((4,)), vmem((size, freqs), f32),
     ]
     out = pl.pallas_call(
         functools.partial(kernel, (n_y, n_z, n_c, n_x)),

time: 107 us -> 107 us (level)
  no operation moved by 1% of the time
where the time goes in v5:
time: 107 us; the launch traced here: 106 us
  Pallas kernels  105 us (98%)
    pallas_call x1, Pallas kernels, shards(): pl.pallas_call(functools.partial(kernel, (n_y, n_z, n_c, n_x)), out_shape...  105 us

profile of v5, /device:TPU:1, one launch (start us, length us, event | category | flops | bytes accessed | tf_op | source)
XLA Modules:
  0.0 106.5 jit_solution(5186537328577979447)
XLA Ops:
  0.0 105.5 %shard_map.46 = f32[64,4096]{1,0:T(8,128)S(1)} custom-call(bf16[256,1024]{1,0:T(8,128)(2,1)} %pupil_hbm.1, s32[1,256]{1,0:T(1,128)} %bitcast.5, s32[2,256]{1,0:T(2,128)} %off_hbm.1, bf16[64,256]{1,0:T(8,128)(2,1)} %bitcast.4), custom_call_target="tpu_custom_call" | custom-call | tf_op jit(solution)/shard_map/pallas_call | solution.py:515
  105.5 1.0 copy.6
